TPU v7x, 256 devices: a whole 4x4x8 slice. The times are simulated.
256 devices in a mesh: ckpt: 4 (over z_lo), tok: 64 (over y, z_hi, x, core).
Axes of the slice: x: 4, y: 4, z: 8 (z_hi: 2, z_lo: 4; z = z_hi * 4 + z_lo), core: 2. Of those that a mesh axis runs over, the one named last changes fastest.
Arguments:
- features: bfloat16 [4, 8192, 1792], P('ckpt', 'tok'), may hold values from -22 to 22
- pairing: int32 [4, 64, 128], P('ckpt', 'tok'), may hold values from 0 to 127, each once within a row
- rotation: bfloat16 [4, 1792, 1792], P('ckpt', 'tok'), may hold values from -1 to 2
Outputs:
- consensus: bfloat16 [8192, 1792], P('tok')
- rotation_next: bfloat16 [4, 1792, 1792], P('ckpt', 'tok')
Inputs may be any that keep to these rules, and one draw needn't show every extreme that they name: Each row of a shard of 128 rows appears once in that shard's pairing.
All inputs are finite; a program needn't handle non-finite values.
Results may differ from a plain program's by a relative error of at most 0.011.
Values may be sent and summed in bfloat16 or wider, within the bound.
A program may use at most 64 MiB of HBM per device.

v0:
```python
import math
import jax
import jax.numpy as jnp
from jax import lax
from jax.sharding import PartitionSpec as P


def apply_once(vector, whole):
    inner = lax.dot_general(
        vector.astype(jnp.bfloat16),
        whole,
        (((1,), (1,)), ((), ())),
        preferred_element_type=jnp.float32,
    ).astype(jnp.bfloat16)
    return jnp.dot(inner, whole, preferred_element_type=jnp.float32)


def normalize(own_cov, feature_width):
    squares = lax.psum(jnp.sum(own_cov * own_cov), "tok")
    return (own_cov / (2.0 * jnp.sqrt(squares / feature_width + 1e-06))).astype(jnp.bfloat16)


def block_form(aligned, consensus, devices, column_groups, send_fn, collect_fn):
    row_count, feature_width = aligned.shape
    row_groups = devices // column_groups
    row_width = feature_width // row_groups
    col_width = feature_width // column_groups
    aligned_cols = jnp.repeat(
        aligned.reshape(row_count, row_groups, row_width).transpose(1, 0, 2), column_groups, axis=0
    ).reshape(devices * row_count, row_width)
    consensus_cols = jnp.tile(
        consensus.reshape(row_count, column_groups, col_width).transpose(1, 0, 2),
        (row_groups, 1, 1),
    ).reshape(devices * row_count, col_width)
    aligned_all, consensus_all = send_fn(aligned_cols, consensus_cols)
    own_cov = lax.dot_general(
        aligned_all, consensus_all, (((0,), (0,)), ((), ())), preferred_element_type=jnp.float32
    )
    start_block = normalize(own_cov, feature_width)
    pieces = collect_fn(start_block)
    return (
        pieces.reshape(row_groups, column_groups, row_width, col_width)
        .transpose(0, 2, 1, 3)
        .reshape(feature_width, feature_width)
    )


def shards(features, pairing, rotation):
    own_rows = features[0]
    own_order = pairing[0, 0]
    rot_rows = rotation[0]
    feature_width = own_rows.shape[1]
    aligned = jnp.take(own_rows, own_order, axis=0)
    rotated = jnp.dot(
        aligned,
        lax.all_gather(rot_rows, "tok", axis=0, tiled=True),
        preferred_element_type=jnp.float32,
    ).astype(jnp.bfloat16)
    summed = lax.psum(rotated.astype(jnp.float32).astype(jnp.bfloat16), "ckpt").astype(jnp.float32)
    consensus = (summed / lax.axis_size("ckpt")).astype(jnp.bfloat16)
    devices = lax.axis_size("tok")
    slab_rows = feature_width // devices

    def send_narrow(left, right):
        return (
            lax.all_to_all(left, "tok", split_axis=0, concat_axis=0, tiled=True),
            lax.all_to_all(right, "tok", split_axis=0, concat_axis=0, tiled=True),
        )

    def collect_narrow(block):
        return lax.all_gather(block, "tok", axis=0, tiled=True)

    whole = block_form(aligned, consensus, devices, min(devices, 8), send_narrow, collect_narrow)
    start_rows = lax.dynamic_slice_in_dim(whole, lax.axis_index("tok") * slab_rows, slab_rows, 0)
    first = 1.5 * start_rows.astype(jnp.float32) - 0.5 * apply_once(start_rows, whole)
    upper = 1.5 * first - 0.5 * apply_once(first, whole)
    middle = apply_once(upper, whole)
    cubic = 1.5 * middle - 0.5 * apply_once(middle, whole)
    rotation_next = (math.sqrt(feature_width) * (1.5 * first - 0.5 * cubic)).astype(jnp.bfloat16)
    return (consensus, rotation_next[None])


def solution(mesh):
    placed = (P("ckpt", "tok", None), P("ckpt", "tok", None), P("ckpt", "tok", None))
    return jax.shard_map(
        shards,
        mesh=mesh,
        in_specs=placed,
        out_specs=(P("tok", None), P("ckpt", "tok", None)),
        check_vma=False,
    )
```

profile of v0, /device:TPU:1, one launch (start us, length us, event | category | flops | bytes accessed | tf_op | source)
XLA Modules:
  0.0 733.9 jit_solution(13692629428495231626)
XLA Ops:
  7.2 0.0 copy-start
  7.2 0.0 all-gather.6.cloned.1.call-start
  7.2 1.8 copy.15
  9.0 0.0 all-gather.6.cloned.1.call-update
  9.0 0.7 fusion.25
  9.7 0.0 copy-done
  9.7 0.9 gather_fusion
  10.6 0.3 copy.16
  10.9 0.7 compare_and_fusion
  11.6 2.4 broadcast_in_dim.24
  14.0 15.8 %all-to-all-start = ((bf16[64,128,224]{1,2,0:T(8,128)(2,1)}), bf16[64,128,224]{1,2,0:T(8,128)(2,1)}, u32[]{:S(2)}, u32[]{:S(2)}) async-start(bf16[64,128,224]{1,2,0:T(8,128)(2,1)} %bitcast.41), calls=%async_computation | async-start | bytes 7340032 | tf_op jit(solution)/shard_map/all_to_all | solution.py:66
  29.7 0.0 all-reduce.2.cloned.1.call-start
  29.8 180.5 %all-gather.6.cloned.1.call-done = bf16[1,1792,1792]{2,0,1:T(2,128)(2,1)} async-done(((bf16[1,28,1792]{2,0,1:T(2,128)(2,1)}), bf16[1,1792,1792]{2,0,1:T(2,128)(2,1)}) %all-gather.6.cloned.1.call-update) | async-done | bytes 6422544 | tf_op jit(solution)/shard_map/all_gather | solution.py:56
  210.3 6.5 fusion.3
  216.8 0.0 all-reduce.2.cloned.1.call-update
  216.8 0.0 all-gather.4.cloned.1.call-start
  216.9 43.3 %all-reduce.2.cloned.1.call-done = bf16[128,1792]{1,0:T(8,128)(2,1)} async-done(((bf16[128,1792]{1,0:T(8,128)(2,1)}), bf16[128,1792]{1,0:T(8,128)(2,1)}) %all-reduce.2.cloned.1.call-update) | async-done | bytes 458768 | tf_op jit(solution)/shard_map/psum | solution.py:59
  260.2 1.1 multiply_convert_fusion
  261.3 0.0 copy-start.1
  261.3 0.3 copy.17
  261.5 0.0 all-to-all-done
  261.5 0.6 tile.8
  262.1 96.3 %all_to_all.15 = bf16[64,128,224]{1,2,0:T(8,128)(2,1)S(1)} all-to-all(bf16[64,128,224]{1,2,0:T(8,128)(2,1)S(1)} %bitcast.42), channel_id=1, replica_groups=mesh['ckpt'=4,'tok'=64] {'tok'}, dimensions={0} | all-to-all | bytes 7340032 | tf_op jit(solution)/shard_map/all_to_all | solution.py:67
  358.4 3.8 multiply_reduce_fusion
  362.2 0.0 copy-done.1
  362.2 191.2 %psum.15 = f32[]{:T(128)} all-reduce(f32[]{:T(128)} %get-tuple-element.2), channel_id=1, replica_groups=mesh['ckpt'=4,'tok'=64] {'tok'}, use_global_device_ids=true, to_apply=%region_2.3 | all-reduce | flops 1 | bytes 8 | tf_op jit(solution)/shard_map/psum | solution.py:19
  554.1 0.7 divide_convert_fusion
  554.8 0.0 all-gather.4.cloned.1.call-update
  554.8 117.2 %all-gather.4.cloned.1.call-done = bf16[14336,224]{1,0:T(8,128)(2,1)} async-done(((bf16[224,224]{1,0:T(8,128)(2,1)}), bf16[14336,224]{1,0:T(8,128)(2,1)}) %all-gather.4.cloned.1.call-update) | async-done | bytes 6422544 | tf_op jit(solution)/shard_map/all_gather | solution.py:71
  672.0 10.5 %copy.18 = bf16[8,224,8,224]{3,2,1,0:T(8,128)(2,1)} copy(bf16[8,224,8,224]{3,1,2,0:T(8,128)(2,1)} %bitcast.43) | data formatting | bytes 12845056 | tf_op jit(solution)/shard_map/transpose | solution.py:43
  682.5 13.7 %reshape.66 = bf16[1792,1792]{1,0:T(8,128)(2,1)} reshape(bf16[8,224,8,224]{3,2,1,0:T(8,128)(2,1)} %copy.18) | data formatting | bytes 12845056 | tf_op jit(solution)/shard_map/reshape | solution.py:44
  696.3 7.7 %fusion.10 = f32[28,1792]{1,0:T(8,128)S(1)} fusion(bf16[1792,1792]{1,0:T(8,128)(2,1)} %reshape.66, s32[]{:T(128)S(6)} %select_n.30), kind=kOutput, calls=%fused_computation.12 | convolution fusion | flops 359912448 | bytes 13276160 | tf_op jit(solution)/shard_map/dot_general | solution.py:15
  704.0 7.6 %fusion.12 = bf16[28,1792]{1,0:T(8,128)(2,1)S(1)} fusion(bf16[1792,1792]{1,0:T(8,128)(2,1)} %reshape.66, f32[28,1792]{1,0:T(8,128)S(1)} %fusion.10), kind=kOutput, calls=%fused_computation.14 | convolution fusion | flops 359962624 | bytes 6723584 | tf_op jit(solution)/shard_map/dot_general | solution.py:15
  711.5 7.6 %fusion.15 = f32[28,1792]{1,0:T(8,128)S(1)} fusion(bf16[1792,1792]{1,0:T(8,128)(2,1)} %reshape.66, bf16[28,1792]{1,0:T(8,128)(2,1)S(1)} %fusion.12), kind=kOutput, calls=%fused_computation.22 | convolution fusion | flops 359711744 | bytes 6723584 | tf_op jit(solution)/shard_map/dot_general | solution.py:15
  719.1 8.2 %fusion.14 = bf16[1,28,1792]{2,1,0:T(8,128)(2,1)} fusion(bf16[1792,1792]{1,0:T(8,128)(2,1)} %reshape.66, f32[28,1792]{1,0:T(8,128)S(1)} %fusion.15, f32[28,1792]{1,0:T(8,128)S(1)} %fusion.10), kind=kOutput, calls=%fused_computation.20 | convolution fusion | flops 360163328 | bytes 6924288 | tf_op jit(solution)/shard_map/dot_general | solution.py:15
  (2 shorter events, 0.1 us)
Async XLA Ops:
  7.2 2.5 copy-start
  7.2 203.1 %all-gather.6.cloned.1.call-start = ((), (), s32[]{:S(2)}) async-start(), calls=%async_computation.4 | async-start | bytes 13045760 | tf_op jit(solution)/shard_map/all_gather | solution.py:56
  14.0 247.6 %all-to-all-start = ((bf16[64,128,224]{1,2,0:T(8,128)(2,1)}), bf16[64,128,224]{1,2,0:T(8,128)(2,1)}, u32[]{:S(2)}, u32[]{:S(2)}) async-start(bf16[64,128,224]{1,2,0:T(8,128)(2,1)} %bitcast.41), calls=%async_computation | async-start | bytes 7340032 | tf_op jit(solution)/shard_map/all_to_all | solution.py:66
  29.7 230.4 %all-reduce.2.cloned.1.call-start = ((), (), s32[]{:S(2)}) async-start(), calls=%async_computation.2 | async-start | bytes 917504 | tf_op jit(solution)/shard_map/psum | solution.py:59
  216.8 455.2 %all-gather.4.cloned.1.call-start = ((), (), s32[]{:S(2)}) async-start(), calls=%async_computation.3 | async-start | bytes 7454720 | tf_op jit(solution)/shard_map/all_gather | solution.py:71
  261.3 101.0 %copy-start.1 = (bf16[128,1792]{1,0:T(8,128)(2,1)}, bf16[128,1792]{1,0:T(8,128)(2,1)S(1)}, u32[]{:S(2)}) copy-start(bf16[128,1792]{1,0:T(8,128)(2,1)S(1)} %multiply_convert_fusion) | copy-start | bytes 1376260
Sparse Core Ops, SparseCore 0:
  12.2 198.0 all-gather.5
  216.9 43.1 all-reduce.1
  555.0 117.0 all-gather.3
where the time goes:
time: 735 us; the launch traced here: 734 us
  waiting for transfers between devices  341 us (46%)
  blocking collectives  288 us (39%)
  matrix products  41.3 us (6%)
  local copies, waits for them, and re-layouts  30.5 us (4%)
  starting transfers between devices  15.9 us (2%)
  between operations  14.5 us (2%)
    psum x1, blocking collectives, normalize(): squares = lax.psum(jnp.sum(own_cov * own_cov), 'tok')  191 us
    all_gather x1, waiting for transfers between devices, shards(): lax.all_gather(rot_rows, 'tok', axis=0, tiled=True)  181 us
    all_gather x1, waiting for transfers between devices, collect_narrow(): return lax.all_gather(block, 'tok', axis=0, tiled=True)  117 us
    all_to_all x1, blocking collectives, send_narrow(): lax.all_to_all(right, 'tok', split_axis=0, concat_axis=0, tiled=True)  96.3 us
    psum x1, waiting for transfers between devices, shards(): lax.psum(rotated.astype(jnp.float32).astype(jnp.bfloat16), 'ckpt')  43.3 us
    dot_general x4, matrix products, apply_once(): return jnp.dot(inner, whole, preferred_element_type=jnp.float32)  31.1 us
    all_to_all x1, starting transfers between devices, send_narrow(): lax.all_to_all(left, 'tok', split_axis=0, concat_axis=0, tiled=True)  15.8 us
  transfers between devices with their start and end apart: 4, of which 3 were waited for; matrix products, arithmetic and copies ran while one was open for 2% of the time, Pallas kernels for 0%

commit v1 on v0

--- a/solution.py
+++ b/solution.py
@@ -3,6 +3,11 @@
 import jax.numpy as jnp
 from jax import lax
 from jax.sharding import PartitionSpec as P
+
+
+def swapped_in(x, axis, along):
+    stack = jnp.stack([x] * lax.axis_size(axis))
+    return jnp.concatenate(lax.all_to_all(stack, axis, 0, 0), axis=along)
 
 
 def apply_once(vector, whole):
@@ -52,9 +57,7 @@
     feature_width = own_rows.shape[1]
     aligned = jnp.take(own_rows, own_order, axis=0)
     rotated = jnp.dot(
-        aligned,
-        lax.all_gather(rot_rows, "tok", axis=0, tiled=True),
-        preferred_element_type=jnp.float32,
+        aligned, swapped_in(rot_rows, "tok", 0), preferred_element_type=jnp.float32
     ).astype(jnp.bfloat16)
     summed = lax.psum(rotated.astype(jnp.float32).astype(jnp.bfloat16), "ckpt").astype(jnp.float32)
     consensus = (summed / lax.axis_size("ckpt")).astype(jnp.bfloat16)

time: 735 us -> 792 us (1.078)
  waiting for transfers between devices: 341 us -> 378 us
  local copies, waits for them, and re-layouts: 30.5 us -> 43.2 us
  starting transfers between devices: 15.9 us -> 25.2 us
    all_gather x1 -> x0, waiting for transfers between devices: 181 us -> none  [shards(): lax.all_gather(rot_rows, 'tok', axis=0, tiled=True)]
    all_to_all x0 -> x1, waiting for transfers between devices: none -> 162 us  [swapped_in(): return jnp.concatenate(lax.all_to_all(stack, axis, 0, 0), axis=along)]
    psum x1, waiting for transfers between devices: 43.3 us -> 99.1 us  [shards(): lax.psum(rotated.astype(jnp.float32).astype(jnp.bfloat16), 'ckpt')]
    all_to_all x0 -> x1, starting transfers between devices: none -> 15.9 us  [swapped_in(): return jnp.concatenate(lax.all_to_all(stack, axis, 0, 0), axis=along)]
    reshape x0 -> x1, local copies, waits for them, and re-layouts: none -> 9.66 us  [swapped_in(): return jnp.concatenate(lax.all_to_all(stack, axis, 0, 0), axis=along)]
where the time goes in v1:
time: 792 us; the launch traced here: 791 us
  waiting for transfers between devices  378 us (48%)
  blocking collectives  288 us (36%)
  local copies, waits for them, and re-layouts  43.2 us (5%)
  matrix products  39.5 us (5%)
  starting transfers between devices  25.2 us (3%)
  between operations  14.8 us (2%)
    psum x1, blocking collectives, normalize(): squares = lax.psum(jnp.sum(own_cov * own_cov), 'tok')  191 us
    all_to_all x1, waiting for transfers between devices, swapped_in(): return jnp.concatenate(lax.all_to_all(stack, axis, 0, 0), axis=along)  162 us
    all_gather x1, waiting for transfers between devices, collect_narrow(): return lax.all_gather(block, 'tok', axis=0, tiled=True)  117 us
    psum x1, waiting for transfers between devices, shards(): lax.psum(rotated.astype(jnp.float32).astype(jnp.bfloat16), 'ckpt')  99.1 us
    all_to_all x1, blocking collectives, send_narrow(): lax.all_to_all(right, 'tok', split_axis=0, concat_axis=0, tiled=True)  96.3 us
    dot_general x4, matrix products, apply_once(): return jnp.dot(inner, whole, preferred_element_type=jnp.float32)  31.1 us
    all_to_all x1, starting transfers between devices, swapped_in(): return jnp.concatenate(lax.all_to_all(stack, axis, 0, 0), axis=along)  15.9 us
  transfers between devices with their start and end apart: 4, of which 3 were waited for; matrix products, arithmetic and copies ran while one was open for 2% of the time, Pallas kernels for 0%

profile of v1, /device:TPU:1, one launch (start us, length us, event | category | flops | bytes accessed | tf_op | source)
XLA Modules:
  0.0 790.5 jit_solution(4595633521866731865)
XLA Ops:
  7.2 0.0 copy-start
  7.2 4.9 stack.3
  12.0 0.0 copy-start.2
  12.0 15.9 %all-to-all-start = ((bf16[64,28,1792]{2,1,0:T(8,128)(2,1)}), bf16[64,28,1792]{2,1,0:T(8,128)(2,1)}, u32[]{:S(2)}, u32[]{:S(2)}) async-start(bf16[64,28,1792]{2,1,0:T(8,128)(2,1)} %stack.3), calls=%async_computation | async-start | bytes 14680064 | tf_op jit(solution)/shard_map/all_to_all | solution.py:10
  28.0 0.0 copy-done.2
  28.0 0.0 copy-done
  28.0 0.9 gather_fusion
  28.9 0.3 copy.8
  29.3 162.1 %all-to-all-done = bf16[64,28,1792]{2,1,0:T(8,128)(2,1)} async-done(((bf16[64,28,1792]{2,1,0:T(8,128)(2,1)}), bf16[64,28,1792]{2,1,0:T(8,128)(2,1)}, u32[]{:S(2)}, u32[]{:S(2)}) %all-to-all-start) | async-done | bytes 6422560 | tf_op jit(solution)/shard_map/all_to_all | solution.py:10
  191.4 2.3 broadcast_in_dim.24
  193.7 9.2 %all-to-all-start.1 = ((bf16[64,128,224]{1,2,0:T(8,128)(2,1)}), bf16[64,128,224]{1,2,0:T(8,128)(2,1)}, u32[]{:S(2)}, u32[]{:S(2)}) async-start(bf16[64,128,224]{1,2,0:T(8,128)(2,1)} %bitcast.38), calls=%async_computation.1 | async-start | bytes 7340032 | tf_op jit(solution)/shard_map/all_to_all | solution.py:69
  202.9 0.0 all-reduce.2.cloned.1.call-start
  203.0 9.7 %reshape.68 = bf16[1792,1792]{1,0:T(8,128)(2,1)} reshape(bf16[64,28,1792]{2,1,0:T(8,128)(2,1)} %all-to-all-done) | data formatting | bytes 12845056 | tf_op jit(solution)/shard_map/reshape | solution.py:10
  212.6 4.7 convolution_convert_fusion
  217.3 0.0 all-reduce.2.cloned.1.call-update
  217.3 0.0 all-gather.2.cloned.1.call-start
  217.4 99.1 %all-reduce.2.cloned.1.call-done = bf16[128,1792]{1,0:T(8,128)(2,1)} async-done(((bf16[128,1792]{1,0:T(8,128)(2,1)}), bf16[128,1792]{1,0:T(8,128)(2,1)}) %all-reduce.2.cloned.1.call-update) | async-done | bytes 458768 | tf_op jit(solution)/shard_map/psum | solution.py:62
  316.5 1.1 multiply_convert_fusion
  317.6 0.0 copy-start.1
  317.6 0.3 copy.9
  317.8 0.0 all-to-all-done.1
  317.9 0.6 tile.8
  318.5 96.3 %all_to_all.20 = bf16[64,128,224]{1,2,0:T(8,128)(2,1)S(1)} all-to-all(bf16[64,128,224]{1,2,0:T(8,128)(2,1)S(1)} %bitcast.39), channel_id=1, replica_groups=mesh['ckpt'=4,'tok'=64] {'tok'}, dimensions={0} | all-to-all | bytes 7340032 | tf_op jit(solution)/shard_map/all_to_all | solution.py:70
  414.8 3.8 multiply_reduce_fusion
  418.5 0.0 copy-done.1
  418.5 191.2 %psum.15 = f32[]{:T(128)} all-reduce(f32[]{:T(128)} %get-tuple-element.2), channel_id=1, replica_groups=mesh['ckpt'=4,'tok'=64] {'tok'}, use_global_device_ids=true, to_apply=%region_2.3 | all-reduce | flops 1 | bytes 8 | tf_op jit(solution)/shard_map/psum | solution.py:24
  610.5 0.7 divide_convert_fusion
  611.1 0.0 all-gather.2.cloned.1.call-update
  611.2 117.2 %all-gather.2.cloned.1.call-done = bf16[14336,224]{1,0:T(8,128)(2,1)} async-done(((bf16[224,224]{1,0:T(8,128)(2,1)}), bf16[14336,224]{1,0:T(8,128)(2,1)}) %all-gather.2.cloned.1.call-update) | async-done | bytes 6422544 | tf_op jit(solution)/shard_map/all_gather | solution.py:74
  728.3 10.5 %copy.10 = bf16[8,224,8,224]{3,2,1,0:T(8,128)(2,1)} copy(bf16[8,224,8,224]{3,1,2,0:T(8,128)(2,1)} %bitcast.40) | data formatting | bytes 12845056 | tf_op jit(solution)/shard_map/transpose | solution.py:48
  738.9 13.7 %reshape.71 = bf16[1792,1792]{1,0:T(8,128)(2,1)} reshape(bf16[8,224,8,224]{3,2,1,0:T(8,128)(2,1)} %copy.10) | data formatting | bytes 12845056 | tf_op jit(solution)/shard_map/reshape | solution.py:49
  752.6 7.7 fusion.4
  760.3 7.6 fusion.6
  767.9 7.6 fusion.9
  775.4 8.2 %fusion.8 = bf16[1,28,1792]{2,1,0:T(8,128)(2,1)} fusion(bf16[1792,1792]{1,0:T(8,128)(2,1)} %reshape.71, f32[28,1792]{1,0:T(8,128)S(1)} %fusion.9, f32[28,1792]{1,0:T(8,128)S(1)} %fusion.4), kind=kOutput, calls=%fused_computation.17 | convolution fusion | flops 360163328 | bytes 6924288 | tf_op jit(solution)/shard_map/dot_general | solution.py:20
  (4 shorter events, 0.1 us)
Async XLA Ops:
  7.2 20.8 %copy-start = (bf16[1,128,1792]{2,1,0:T(8,128)(2,1)S(1)}, bf16[1,128,1792]{2,1,0:T(8,128)(2,1)}, u32[]{:S(2)}) copy-start(bf16[1,128,1792]{2,1,0:T(8,128)(2,1)} %param.3) | copy-start | bytes 1376260
  12.0 15.9 %copy-start.2 = (s32[1,1,128]{2,1,0:T(1,128)S(1)}, s32[1,1,128]{2,1,0:T(1,128)}, u32[]{:S(2)}) copy-start(s32[1,1,128]{2,1,0:T(1,128)} %param.4) | copy-start | bytes 1540
  12.0 179.4 %all-to-all-start = ((bf16[64,28,1792]{2,1,0:T(8,128)(2,1)}), bf16[64,28,1792]{2,1,0:T(8,128)(2,1)}, u32[]{:S(2)}, u32[]{:S(2)}) async-start(bf16[64,28,1792]{2,1,0:T(8,128)(2,1)} %stack.3), calls=%async_computation | async-start | bytes 14680064 | tf_op jit(solution)/shard_map/all_to_all | solution.py:10
  193.7 124.1 %all-to-all-start.1 = ((bf16[64,128,224]{1,2,0:T(8,128)(2,1)}), bf16[64,128,224]{1,2,0:T(8,128)(2,1)}, u32[]{:S(2)}, u32[]{:S(2)}) async-start(bf16[64,128,224]{1,2,0:T(8,128)(2,1)} %bitcast.38), calls=%async_computation.1 | async-start | bytes 7340032 | tf_op jit(solution)/shard_map/all_to_all | solution.py:69
  202.9 113.6 %all-reduce.2.cloned.1.call-start = ((), (), s32[]{:S(2)}) async-start(), calls=%async_computation.3 | async-start | bytes 917504 | tf_op jit(solution)/shard_map/psum | solution.py:62
  217.3 511.0 %all-gather.2.cloned.1.call-start = ((), (), s32[]{:S(2)}) async-start(), calls=%async_computation.4 | async-start | bytes 7454720 | tf_op jit(solution)/shard_map/all_gather | solution.py:74
  317.6 101.0 %copy-start.1 = (bf16[128,1792]{1,0:T(8,128)(2,1)}, bf16[128,1792]{1,0:T(8,128)(2,1)S(1)}, u32[]{:S(2)}) copy-start(bf16[128,1792]{1,0:T(8,128)(2,1)S(1)} %multiply_convert_fusion) | copy-start | bytes 1376260
Sparse Core Ops, SparseCore 0:
  217.4 99.0 all-reduce.1
  611.3 117.0 all-gather.1
